TPU v7x, 256 devices: a whole 4x4x8 slice. The times are simulated.
256 devices in a mesh: kv: 2 (over core), seq: 128 (over z, y, x).
Axes of the slice: x: 4, y: 4, z: 8, core: 2. Of those that a mesh axis runs over, the one named last changes fastest.
Arguments:
- tokens: bfloat16 [32768, 4096], P(('seq', 'kv')), may hold values from -6 to 6
- gain: float32 [4096], replicated, may hold values from 0.25 to 1.75
- w_query: bfloat16 [4096, 4096], P(None, 'kv'), may hold values from -1 to 1
- w_key: bfloat16 [4096, 1024], P(None, 'kv'), may hold values from -4 to 4
- w_value: bfloat16 [4096, 1024], P(None, 'kv'), may hold values from -0.09375 to 0.09375
- w_out: bfloat16 [4096, 4096], P('kv'), may hold values from -0.09375 to 0.09375
- segment_ids: int32 [32768], replicated, may hold values from 0 to 32767, as said below
- page_table: int32 [256], P('seq'), may hold values from 0 to 1, as said below
Outputs:
- mixed: bfloat16 [32768, 4096], P(('seq', 'kv'))
- attn_out: bfloat16 [32768, 4096], P(('seq', 'kv'))
- page_pool: bfloat16 [256, 2, 8, 128, 128], P('seq', None, 'kv')
Inputs may be any that keep to these rules, and one draw needn't show every extreme that they name: `segment_ids`: never falls along the stream; tokens of one prompt share the position of its first token as id; every prompt has 1 to 2048 tokens; exactly two prompts have 2048 tokens, one in each half of the stream, each beginning inside a block of 256 tokens and not at its first token; every other prompt has fewer than 128 tokens; the last token of the stream is a prompt of its own. `page_table`: in each aligned block of 2 entries every value appears once.
All inputs are finite; a program needn't handle non-finite values.
Results may differ from a plain program's by a relative error of at most 0.0065.
The roundings to bfloat16 on the way count: a program that leaves them out, or rounds other values in their place, can miss the bound.
Values may be sent and summed in bfloat16 or wider, within the bound.
A program may use at most 192 MiB of HBM per device.

v0:
```python
from functools import partial
import jax
import jax.numpy as jnp
from jax import lax
from jax.sharding import PartitionSpec as P

HD = 128
norm_eps = 1e-05


def shifted(value, axis, steps):
    count = lax.axis_size(axis)
    leading, last = (max(0, -steps), min(count, count - steps))
    return lax.ppermute(value, axis, [(source, source + steps) for source in range(leading, last)])


def head_attention(inputs, masks, live, sparse):
    query_head, key_blocks, value_blocks = inputs
    block_count = key_blocks.shape[0]
    key_width = key_blocks.shape[1]
    score_scale = query_head.shape[-1] ** (-0.5)

    def block_scores(distance):
        scores = (
            jnp.einsum(
                "qgd,kd->gqk", query_head, key_blocks[distance], preferred_element_type=jnp.float32
            )
            * score_scale
        )
        return jnp.where(masks[distance][None], scores, -jnp.inf)

    pieces = [block_scores(0)]
    for distance in range(1, block_count):
        pieces.append(block_scores(distance))
    scores = jnp.concatenate(pieces, axis=2)
    row_peak = jnp.max(scores, axis=2, keepdims=True)
    weights = jnp.exp(scores - row_peak).astype(jnp.bfloat16)
    row_total = jnp.sum(weights, axis=2, dtype=jnp.float32)
    all_values = value_blocks.reshape(block_count * key_width, value_blocks.shape[-1])
    weighted = jnp.einsum("gqk,kd->qgd", weights, all_values, preferred_element_type=jnp.float32)
    return (weighted / row_total.T[:, :, None]).astype(jnp.bfloat16)


def shards(tokens, gain, w_query, w_key, w_value, w_out, segment_ids, page_table):
    tok_rows = tokens.shape[0]
    block_rows = tok_rows * lax.axis_size("kv")
    reach = min(8, lax.axis_size("seq") // 2 - 1)
    kv_local = w_key.shape[1] // HD
    q_local = w_query.shape[1] // HD
    group_size = q_local // kv_local
    wide_rows = tokens.astype(jnp.float32)
    normed = (
        wide_rows
        * lax.rsqrt(jnp.mean(wide_rows * wide_rows, axis=1, keepdims=True) + norm_eps)
        * gain
    ).astype(jnp.bfloat16)
    piece = lax.all_gather(normed, "kv", axis=0, tiled=True)
    projected = jnp.concatenate(
        [
            jnp.dot(piece, w_query, preferred_element_type=jnp.float32),
            jnp.dot(piece, w_key, preferred_element_type=jnp.float32),
            jnp.dot(piece, w_value, preferred_element_type=jnp.float32),
        ],
        axis=1,
    ).astype(jnp.bfloat16)
    query_cols = q_local * HD
    key_cols = kv_local * HD
    query = projected[:, :query_cols].reshape(block_rows, kv_local, group_size, HD)
    key_rows = projected[:, query_cols : query_cols + key_cols].reshape(block_rows, kv_local, HD)
    value_rows = projected[:, query_cols + key_cols :].reshape(block_rows, kv_local, HD)
    pair_rows = jnp.stack([key_rows, value_rows], axis=0)
    page_rows = page_table.shape[0]
    page_len = block_rows // page_rows
    pages = pair_rows.reshape(2, page_rows, page_len, kv_local, HD).transpose(1, 0, 3, 2, 4)
    page_pool = jnp.zeros_like(pages).at[page_table].set(pages)
    received = [pair_rows]
    carried = pair_rows
    for distance in range(1, reach + 1):
        carried = shifted(carried, "seq", 1)
        received.append(carried)
    stacked_pairs = jnp.stack(received, axis=1)
    seq_index = lax.axis_index("seq")
    query_segs = lax.dynamic_slice_in_dim(segment_ids, seq_index * block_rows, block_rows)
    lower = jnp.arange(block_rows)[None, :] <= jnp.arange(block_rows)[:, None]
    mask_list = []
    live_list = []
    for distance in range(reach + 1):
        source = jnp.maximum(seq_index - distance, 0)
        valid = seq_index - distance >= 0
        key_segs = lax.dynamic_slice_in_dim(segment_ids, source * block_rows, block_rows)
        same = (key_segs[None, :] == query_segs[:, None]) & valid
        if distance == 0:
            same = same & lower
            live_list.append(jnp.array(True))
        else:
            live_list.append(valid & (key_segs[block_rows - 1] == query_segs[0]))
        mask_list.append(same)
    masks = jnp.stack(mask_list)
    live = jnp.stack(live_list)
    heads_out = lax.map(
        partial(head_attention, masks=masks, live=live, sparse=False),
        (
            query.transpose(1, 0, 2, 3),
            stacked_pairs[0].transpose(2, 0, 1, 3),
            stacked_pairs[1].transpose(2, 0, 1, 3),
        ),
    )
    attention = heads_out.transpose(1, 0, 2, 3).reshape(block_rows, q_local * HD)
    summed = lax.psum(jnp.dot(attention, w_out, preferred_element_type=jnp.float32), "kv")
    branch = lax.dynamic_slice_in_dim(summed, lax.axis_index("kv") * tok_rows, tok_rows, 0)
    attn_out = branch.astype(jnp.bfloat16)
    mixed = (wide_rows + branch).astype(jnp.bfloat16)
    return (mixed, attn_out, page_pool)


def solution(mesh):
    in_specs = (
        P(("seq", "kv"), None),
        P(),
        P(None, "kv"),
        P(None, "kv"),
        P(None, "kv"),
        P("kv", None),
        P(),
        P("seq"),
    )
    out_specs = (P(("seq", "kv"), None), P(("seq", "kv"), None), P("seq", None, "kv", None, None))
    return jax.shard_map(shards, mesh=mesh, in_specs=in_specs, out_specs=out_specs, check_vma=False)
```

profile of v0, /device:TPU:1, one launch (start us, length us, event | category | flops | bytes accessed | tf_op | source)
XLA Modules:
  0.0 373.4 jit_solution(7717644761476916831)
XLA Ops:
  11.3 20.5 %all-gather.2.cloned.1.call-done = bf16[256,4096]{1,0:T(8,128)(2,1)} async-done(((bf16[128,4096]{1,0:T(8,128)(2,1)}), bf16[256,4096]{1,0:T(8,128)(2,1)}) %all-gather.2.cloned.1.call-update) | async-done | bytes 2097168 | tf_op jit(solution)/shard_map/all_gather | solution.py:57
  31.9 4.1 %convolution_convert_fusion.2 = bf16[256,512]{1,0:T(8,128)(2,1)S(1)} fusion(bf16[256,4096]{1,0:T(8,128)(2,1)} %all-gather.2.cloned.1.call-done, bf16[4096,512]{1,0:T(8,128)(2,1)} %param.13), kind=kOutput, calls=%fused_computation.115 | convolution fusion | flops 1073872896 | bytes 6553600 | tf_op jit(solution)/shard_map/dot_general | solution.py:61
  36.1 4.1 %convolution_convert_fusion.1 = bf16[256,512]{1,0:T(8,128)(2,1)S(1)} fusion(bf16[256,4096]{1,0:T(8,128)(2,1)} %all-gather.2.cloned.1.call-done, bf16[4096,512]{1,0:T(8,128)(2,1)} %param.14), kind=kOutput, calls=%fused_computation.114 | convolution fusion | flops 1073872896 | bytes 6553600 | tf_op jit(solution)/shard_map/dot_general | solution.py:62
  43.1 11.0 %collective-permute-done = bf16[2,256,4,128]{3,1,2,0:T(8,128)(2,1)S(1)} collective-permute-done((bf16[2,256,4,128]{3,1,2,0:T(8,128)(2,1)S(1)}, bf16[2,256,4,128]{3,1,2,0:T(8,128)(2,1)S(1)}, u32[]{:S(2)}, u32[]{:S(2)}) %collective-permute-start) | collective-permute-done | bytes 524320 | tf_op jit(solution)/shard_map/ppermute | solution.py:14
  54.1 4.1 %collective-permute-start.1 = (bf16[2,256,4,128]{3,1,2,0:T(8,128)(2,1)S(1)}, bf16[2,256,4,128]{3,1,2,0:T(8,128)(2,1)S(1)}, u32[]{:S(2)}, u32[]{:S(2)}) collective-permute-start(bf16[2,256,4,128]{3,1,2,0:T(8,128)(2,1)S(1)} %collective-permute-done), channel_id=1, source_target_pairs={{0,1},{1,2},{2,3},{3,4},{4,5},{5,6},{6,7},{7,8},{8,9},{9,10},{10,1... | collective-permute-start | bytes 1572872 | tf_op jit(solution)/shard_map/ppermute | solution.py:14
  58.3 10.2 %collective-permute-done.1 = bf16[2,256,4,128]{3,1,2,0:T(8,128)(2,1)S(1)} collective-permute-done((bf16[2,256,4,128]{3,1,2,0:T(8,128)(2,1)S(1)}, bf16[2,256,4,128]{3,1,2,0:T(8,128)(2,1)S(1)}, u32[]{:S(2)}, u32[]{:S(2)}) %collective-permute-start.1) | collective-permute-done | bytes 524320 | tf_op jit(solution)/shard_map/ppermute | solution.py:14
  68.4 4.1 %collective-permute-start.2 = (bf16[2,256,4,128]{3,1,2,0:T(8,128)(2,1)S(1)}, bf16[2,256,4,128]{3,1,2,0:T(8,128)(2,1)S(1)}, u32[]{:S(2)}, u32[]{:S(2)}) collective-permute-start(bf16[2,256,4,128]{3,1,2,0:T(8,128)(2,1)S(1)} %collective-permute-done.1), channel_id=1, source_target_pairs={{0,1},{1,2},{2,3},{3,4},{4,5},{5,6},{6,7},{7,8},{8,9},{9,10},{10,1... | collective-permute-start | bytes 1572872 | tf_op jit(solution)/shard_map/ppermute | solution.py:14
  72.6 9.3 %collective-permute-done.2 = bf16[2,256,4,128]{3,1,2,0:T(8,128)(2,1)S(1)} collective-permute-done((bf16[2,256,4,128]{3,1,2,0:T(8,128)(2,1)S(1)}, bf16[2,256,4,128]{3,1,2,0:T(8,128)(2,1)S(1)}, u32[]{:S(2)}, u32[]{:S(2)}) %collective-permute-start.2) | collective-permute-done | bytes 524320 | tf_op jit(solution)/shard_map/ppermute | solution.py:14
  82.7 4.1 %collective-permute-start.3 = (bf16[2,256,4,128]{3,1,2,0:T(8,128)(2,1)S(1)}, bf16[2,256,4,128]{3,1,2,0:T(8,128)(2,1)S(1)}, u32[]{:S(2)}, u32[]{:S(2)}) collective-permute-start(bf16[2,256,4,128]{3,1,2,0:T(8,128)(2,1)S(1)} %collective-permute-done.2), channel_id=1, source_target_pairs={{0,1},{1,2},{2,3},{3,4},{4,5},{5,6},{6,7},{7,8},{8,9},{9,10},{10,1... | collective-permute-start | bytes 1572872 | tf_op jit(solution)/shard_map/ppermute | solution.py:14
  86.8 8.4 %collective-permute-done.3 = bf16[2,256,4,128]{3,1,2,0:T(8,128)(2,1)S(1)} collective-permute-done((bf16[2,256,4,128]{3,1,2,0:T(8,128)(2,1)S(1)}, bf16[2,256,4,128]{3,1,2,0:T(8,128)(2,1)S(1)}, u32[]{:S(2)}, u32[]{:S(2)}) %collective-permute-start.3) | collective-permute-done | bytes 524320 | tf_op jit(solution)/shard_map/ppermute | solution.py:14
  95.2 4.9 %collective-permute-start.4 = (bf16[2,256,4,128]{3,1,2,0:T(8,128)(2,1)S(1)}, bf16[2,256,4,128]{3,1,2,0:T(8,128)(2,1)}, u32[]{:S(2)}, u32[]{:S(2)}) collective-permute-start(bf16[2,256,4,128]{3,1,2,0:T(8,128)(2,1)S(1)} %collective-permute-done.3), channel_id=1, source_target_pairs={{0,1},{1,2},{2,3},{3,4},{4,5},{5,6},{6,7},{7,8},{8,9},{9,10},{10,1... | collective-permute-start | bytes 1572872 | tf_op jit(solution)/shard_map/ppermute | solution.py:14
  101.3 5.7 %collective-permute-done.4 = bf16[2,256,4,128]{3,1,2,0:T(8,128)(2,1)} collective-permute-done((bf16[2,256,4,128]{3,1,2,0:T(8,128)(2,1)S(1)}, bf16[2,256,4,128]{3,1,2,0:T(8,128)(2,1)}, u32[]{:S(2)}, u32[]{:S(2)}) %collective-permute-start.4) | collective-permute-done | bytes 524320 | tf_op jit(solution)/shard_map/ppermute | solution.py:14
  107.0 5.8 %collective-permute-start.5 = (bf16[2,256,4,128]{3,1,2,0:T(8,128)(2,1)}, bf16[2,256,4,128]{3,1,2,0:T(8,128)(2,1)}, u32[]{:S(2)}, u32[]{:S(2)}) collective-permute-start(bf16[2,256,4,128]{3,1,2,0:T(8,128)(2,1)} %collective-permute-done.4), channel_id=1, source_target_pairs={{0,1},{1,2},{2,3},{3,4},{4,5},{5,6},{6,7},{7,8},{8,9},{9,10},{10,1... | collective-permute-start | bytes 1572872 | tf_op jit(solution)/shard_map/ppermute | solution.py:14
  112.8 10.9 %convolution_convert_fusion = bf16[256,2048]{1,0:T(8,128)(2,1)S(1)} fusion(bf16[256,4096]{1,0:T(8,128)(2,1)} %all-gather.2.cloned.1.call-done, bf16[4096,2048]{1,0:T(8,128)(2,1)} %param.12), kind=kOutput, calls=%fused_computation.106 | convolution fusion | flops 4295491584 | bytes 19922944 | tf_op jit(solution)/shard_map/dot_general | solution.py:60
  126.9 5.5 %collective-permute-start.6 = (bf16[2,256,4,128]{3,1,2,0:T(8,128)(2,1)}, bf16[2,256,4,128]{3,1,2,0:T(8,128)(2,1)S(1)}, u32[]{:S(2)}, u32[]{:S(2)}) collective-permute-start(bf16[2,256,4,128]{3,1,2,0:T(8,128)(2,1)} %collective-permute-done.5), channel_id=1, source_target_pairs={{0,1},{1,2},{2,3},{3,4},{4,5},{5,6},{6,7},{7,8},{8,9},{9,10},{10,1... | collective-permute-start | bytes 1572872 | tf_op jit(solution)/shard_map/ppermute | solution.py:14
  133.6 5.5 %collective-permute-done.6 = bf16[2,256,4,128]{3,1,2,0:T(8,128)(2,1)S(1)} collective-permute-done((bf16[2,256,4,128]{3,1,2,0:T(8,128)(2,1)}, bf16[2,256,4,128]{3,1,2,0:T(8,128)(2,1)S(1)}, u32[]{:S(2)}, u32[]{:S(2)}) %collective-permute-start.6) | collective-permute-done | bytes 524320 | tf_op jit(solution)/shard_map/ppermute | solution.py:14
  139.1 6.4 %collective-permute-start.7 = (bf16[2,256,4,128]{3,1,2,0:T(8,128)(2,1)S(1)}, bf16[2,256,4,128]{3,1,2,0:T(8,128)(2,1)S(1)}, u32[]{:S(2)}, u32[]{:S(2)}) collective-permute-start(bf16[2,256,4,128]{3,1,2,0:T(8,128)(2,1)S(1)} %collective-permute-done.6), channel_id=1, source_target_pairs={{0,1},{1,2},{2,3},{3,4},{4,5},{5,6},{6,7},{7,8},{8,9},{9,10},{10,1... | collective-permute-start | bytes 1572872 | tf_op jit(solution)/shard_map/ppermute | solution.py:14
  153.2 120.6 %while.12 = (s32[]{:T(128)}, bf16[4,256,4,128]{1,3,2,0:T(8,128)(2,1)}, bf16[4,9,256,128]{3,2,1,0:T(8,128)(2,1)S(1)}, bf16[4,9,256,128]{3,2,1,0:T(8,128)(2,1)}, b...) while((s32[]{:T(128)}, ...), condition=%wide.region_12.13_spmd.clone.clone, body=%wide.region_1.12_spmd.clone.clone.sunk | while | flops 1230764032 | bytes 72335304 | solution.py:100
  174.6 5.1 %convert_reduce_fusion.2 = f32[4,256]{1,0:T(4,128)S(1)} fusion(f32[4,256,2304]{1,2,0:T(8,128)} %get-tuple-element.530, f32[4,256]{1,0:T(4,128)S(1)} %maximum_maximum_fusion.2), kind=kLoop, calls=%fused_computation.10.clone.1 | loop fusion | flops 9436160 | bytes 9445376 | tf_op jit(solution)/shard_map/while/body/eval_jaxpr/reduce_sum | solution.py:38
  204.7 5.1 %convert_reduce_fusion.2 = f32[4,256]{1,0:T(4,128)S(1)} fusion(f32[4,256,2304]{1,2,0:T(8,128)} %get-tuple-element.530, f32[4,256]{1,0:T(4,128)S(1)} %maximum_maximum_fusion.2), kind=kLoop, calls=%fused_computation.10.clone.1 | loop fusion | flops 9436160 | bytes 9445376 | tf_op jit(solution)/shard_map/while/body/eval_jaxpr/reduce_sum | solution.py:38
  234.9 5.1 %convert_reduce_fusion.2 = f32[4,256]{1,0:T(4,128)S(1)} fusion(f32[4,256,2304]{1,2,0:T(8,128)} %get-tuple-element.530, f32[4,256]{1,0:T(4,128)S(1)} %maximum_maximum_fusion.2), kind=kLoop, calls=%fused_computation.10.clone.1 | loop fusion | flops 9436160 | bytes 9445376 | tf_op jit(solution)/shard_map/while/body/eval_jaxpr/reduce_sum | solution.py:38
  265.0 5.1 %convert_reduce_fusion.2 = f32[4,256]{1,0:T(4,128)S(1)} fusion(f32[4,256,2304]{1,2,0:T(8,128)} %get-tuple-element.530, f32[4,256]{1,0:T(4,128)S(1)} %maximum_maximum_fusion.2), kind=kLoop, calls=%fused_computation.10.clone.1 | loop fusion | flops 9436160 | bytes 9445376 | tf_op jit(solution)/shard_map/while/body/eval_jaxpr/reduce_sum | solution.py:38
  273.8 12.7 %fusion.85 = f32[256,4096]{1,0:T(8,128)} fusion(bf16[256,2048]{0,1:T(8,128)(2,1)} %bitcast.280, bf16[2048,4096]{1,0:T(8,128)(2,1)} %param.15), kind=kOutput, calls=%fused_computation.141 | convolution fusion | flops 4294967296 | bytes 22020096 | tf_op jit(solution)/shard_map/dot_general | solution.py:109
  287.7 73.3 %all-reduce.2.cloned.1.call-done = f32[256,4096]{1,0:T(8,128)} async-done(((f32[256,4096]{1,0:T(8,128)}), f32[256,4096]{1,0:T(8,128)}) %all-reduce.2.cloned.1.call-update) | async-done | bytes 4194320 | tf_op jit(solution)/shard_map/psum | solution.py:109
  (116 shorter events, 128.1 us)
Async XLA Ops:
  7.2 24.7 %all-gather.2.cloned.1.call-start = ((), (), s32[]{:S(2)}) async-start(), calls=%async_computation | async-start | bytes 3145728 | tf_op jit(solution)/shard_map/all_gather | solution.py:57
  11.3 349.8 %all-reduce.2.cloned.1.call-start = ((), (), s32[]{:S(2)}) async-start(), calls=%async_computation.1 | async-start | bytes 8388608 | tf_op jit(solution)/shard_map/psum | solution.py:109
  40.3 13.9 %collective-permute-start = (bf16[2,256,4,128]{3,1,2,0:T(8,128)(2,1)S(1)}, bf16[2,256,4,128]{3,1,2,0:T(8,128)(2,1)S(1)}, u32[]{:S(2)}, u32[]{:S(2)}) collective-permute-start(bf16[2,256,4,128]{3,1,2,0:T(8,128)(2,1)S(1)} %copy_dynamic-update-slice_fusion), channel_id=1, source_target_pairs={{0,1},{1,2},{2,3},{3,4},{4,5},{5,6},{6,7},{7,8},{8,9},{9,10},{10,1... | collective-permute-start | bytes 1572872 | tf_op jit(solution)/shard_map/ppermute | solution.py:14
  54.1 52.8 %copy-start.4 = (bf16[2,256,4,128]{3,1,2,0:T(8,128)(2,1)}, bf16[2,256,4,128]{3,1,2,0:T(8,128)(2,1)S(1)}, u32[]{:S(2)}) copy-start(bf16[2,256,4,128]{3,1,2,0:T(8,128)(2,1)S(1)} %collective-permute-done) | copy-start | bytes 1572868
  54.1 14.3 %collective-permute-start.1 = (bf16[2,256,4,128]{3,1,2,0:T(8,128)(2,1)S(1)}, bf16[2,256,4,128]{3,1,2,0:T(8,128)(2,1)S(1)}, u32[]{:S(2)}, u32[]{:S(2)}) collective-permute-start(bf16[2,256,4,128]{3,1,2,0:T(8,128)(2,1)S(1)} %collective-permute-done), channel_id=1, source_target_pairs={{0,1},{1,2},{2,3},{3,4},{4,5},{5,6},{6,7},{7,8},{8,9},{9,10},{10,1... | collective-permute-start | bytes 1572872 | tf_op jit(solution)/shard_map/ppermute | solution.py:14
  68.4 38.5 %copy-start.3 = (bf16[2,256,4,128]{3,1,2,0:T(8,128)(2,1)}, bf16[2,256,4,128]{3,1,2,0:T(8,128)(2,1)S(1)}, u32[]{:S(2)}) copy-start(bf16[2,256,4,128]{3,1,2,0:T(8,128)(2,1)S(1)} %collective-permute-done.1) | copy-start | bytes 1572868
  68.4 13.4 %collective-permute-start.2 = (bf16[2,256,4,128]{3,1,2,0:T(8,128)(2,1)S(1)}, bf16[2,256,4,128]{3,1,2,0:T(8,128)(2,1)S(1)}, u32[]{:S(2)}, u32[]{:S(2)}) collective-permute-start(bf16[2,256,4,128]{3,1,2,0:T(8,128)(2,1)S(1)} %collective-permute-done.1), channel_id=1, source_target_pairs={{0,1},{1,2},{2,3},{3,4},{4,5},{5,6},{6,7},{7,8},{8,9},{9,10},{10,1... | collective-permute-start | bytes 1572872 | tf_op jit(solution)/shard_map/ppermute | solution.py:14
  81.9 0.8 copy-start.5
  82.7 12.6 %collective-permute-start.3 = (bf16[2,256,4,128]{3,1,2,0:T(8,128)(2,1)S(1)}, bf16[2,256,4,128]{3,1,2,0:T(8,128)(2,1)S(1)}, u32[]{:S(2)}, u32[]{:S(2)}) collective-permute-start(bf16[2,256,4,128]{3,1,2,0:T(8,128)(2,1)S(1)} %collective-permute-done.2), channel_id=1, source_target_pairs={{0,1},{1,2},{2,3},{3,4},{4,5},{5,6},{6,7},{7,8},{8,9},{9,10},{10,1... | collective-permute-start | bytes 1572872 | tf_op jit(solution)/shard_map/ppermute | solution.py:14
  95.2 17.5 %copy-start.7 = (bf16[2,256,4,128]{3,1,2,0:T(8,128)(2,1)}, bf16[2,256,4,128]{3,1,2,0:T(8,128)(2,1)S(1)}, u32[]{:S(2)}) copy-start(bf16[2,256,4,128]{3,1,2,0:T(8,128)(2,1)S(1)} %collective-permute-done.3) | copy-start | bytes 1572868
  95.2 11.7 %collective-permute-start.4 = (bf16[2,256,4,128]{3,1,2,0:T(8,128)(2,1)S(1)}, bf16[2,256,4,128]{3,1,2,0:T(8,128)(2,1)}, u32[]{:S(2)}, u32[]{:S(2)}) collective-permute-start(bf16[2,256,4,128]{3,1,2,0:T(8,128)(2,1)S(1)} %collective-permute-done.3), channel_id=1, source_target_pairs={{0,1},{1,2},{2,3},{3,4},{4,5},{5,6},{6,7},{7,8},{8,9},{9,10},{10,1... | collective-permute-start | bytes 1572872 | tf_op jit(solution)/shard_map/ppermute | solution.py:14
  107.0 19.9 %collective-permute-start.5 = (bf16[2,256,4,128]{3,1,2,0:T(8,128)(2,1)}, bf16[2,256,4,128]{3,1,2,0:T(8,128)(2,1)}, u32[]{:S(2)}, u32[]{:S(2)}) collective-permute-start(bf16[2,256,4,128]{3,1,2,0:T(8,128)(2,1)} %collective-permute-done.4), channel_id=1, source_target_pairs={{0,1},{1,2},{2,3},{3,4},{4,5},{5,6},{6,7},{7,8},{8,9},{9,10},{10,1... | collective-permute-start | bytes 1572872 | tf_op jit(solution)/shard_map/ppermute | solution.py:14
  124.4 9.0 %copy-start.6 = (bf16[2,256,4,128]{3,1,2,0:T(8,128)(2,1)S(1)}, bf16[2,256,4,128]{3,1,2,0:T(8,128)(2,1)}, u32[]{:S(2)}) copy-start(bf16[2,256,4,128]{3,1,2,0:T(8,128)(2,1)} %copy-done.5) | copy-start | bytes 1572868
  124.4 9.1 %copy-start.8 = (bf16[2,256,4,128]{3,1,2,0:T(8,128)(2,1)S(1)}, bf16[2,256,4,128]{3,1,2,0:T(8,128)(2,1)}, u32[]{:S(2)}) copy-start(bf16[2,256,4,128]{3,1,2,0:T(8,128)(2,1)} %copy-done.7) | copy-start | bytes 1572868
  126.9 12.2 %collective-permute-start.6 = (bf16[2,256,4,128]{3,1,2,0:T(8,128)(2,1)}, bf16[2,256,4,128]{3,1,2,0:T(8,128)(2,1)S(1)}, u32[]{:S(2)}, u32[]{:S(2)}) collective-permute-start(bf16[2,256,4,128]{3,1,2,0:T(8,128)(2,1)} %collective-permute-done.5), channel_id=1, source_target_pairs={{0,1},{1,2},{2,3},{3,4},{4,5},{5,6},{6,7},{7,8},{8,9},{9,10},{10,1... | collective-permute-start | bytes 1572872 | tf_op jit(solution)/shard_map/ppermute | solution.py:14
  139.1 12.3 %collective-permute-start.7 = (bf16[2,256,4,128]{3,1,2,0:T(8,128)(2,1)S(1)}, bf16[2,256,4,128]{3,1,2,0:T(8,128)(2,1)S(1)}, u32[]{:S(2)}, u32[]{:S(2)}) collective-permute-start(bf16[2,256,4,128]{3,1,2,0:T(8,128)(2,1)S(1)} %collective-permute-done.6), channel_id=1, source_target_pairs={{0,1},{1,2},{2,3},{3,4},{4,5},{5,6},{6,7},{7,8},{8,9},{9,10},{10,1... | collective-permute-start | bytes 1572872 | tf_op jit(solution)/shard_map/ppermute | solution.py:14
  174.6 6.4 %copy-start = (f32[4,256,2304]{1,2,0:T(8,128)S(1)}, f32[4,256,2304]{1,2,0:T(8,128)}, u32[]{:S(2)}) copy-start(f32[4,256,2304]{1,2,0:T(8,128)} %get-tuple-element.530) | copy-start | bytes 28311556 | tf_op jit(solution)/shard_map/while
  204.7 6.4 %copy-start = (f32[4,256,2304]{1,2,0:T(8,128)S(1)}, f32[4,256,2304]{1,2,0:T(8,128)}, u32[]{:S(2)}) copy-start(f32[4,256,2304]{1,2,0:T(8,128)} %get-tuple-element.530) | copy-start | bytes 28311556 | tf_op jit(solution)/shard_map/while
  234.9 6.4 %copy-start = (f32[4,256,2304]{1,2,0:T(8,128)S(1)}, f32[4,256,2304]{1,2,0:T(8,128)}, u32[]{:S(2)}) copy-start(f32[4,256,2304]{1,2,0:T(8,128)} %get-tuple-element.530) | copy-start | bytes 28311556 | tf_op jit(solution)/shard_map/while
  265.0 6.4 %copy-start = (f32[4,256,2304]{1,2,0:T(8,128)S(1)}, f32[4,256,2304]{1,2,0:T(8,128)}, u32[]{:S(2)}) copy-start(f32[4,256,2304]{1,2,0:T(8,128)} %get-tuple-element.530) | copy-start | bytes 28311556 | tf_op jit(solution)/shard_map/while
  273.8 12.7 %copy-start.9 = (s32[2]{0:T(128)S(1)}, s32[2]{0:T(128)}, u32[]{:S(2)}) copy-start(s32[2]{0:T(128)} %param.17) | copy-start | bytes 28
  286.5 77.2 %copy-start.1 = (bf16[128,4096]{1,0:T(8,128)(2,1)S(1)}, bf16[128,4096]{1,0:T(8,128)(2,1)}, u32[]{:S(2)}) copy-start(bf16[128,4096]{1,0:T(8,128)(2,1)} %param.10) | copy-start | bytes 3145732
  287.7 78.8 %copy-start.2 = (bf16[2,2,4,128,128]{4,3,2,1,0:T(8,128)(2,1)}, bf16[2,2,4,128,128]{4,3,2,1,0:T(8,128)(2,1)S(1)}, u32[]{:S(2)}) copy-start(bf16[2,2,4,128,128]{4,3,2,1,0:T(8,128)(2,1)S(1)} %scatter_fusion) | copy-start | bytes 1572868
Sparse Core Ops, SparseCore 0:
  11.4 20.4 all-gather.1
  286.6 74.3 all-reduce.1
where the time goes:
time: 375 us; the launch traced here: 373 us
  waiting for transfers between devices  148 us (39%)
  matrix products  124 us (33%)
  starting transfers between devices  37.9 us (10%)
  other arithmetic  29.6 us (8%)
  local copies, waits for them, and re-layouts  19.6 us (5%)
  between operations  14.3 us (4%)
    dot_general x36, matrix products, block_scores(): jnp.einsum('qgd,kd->gqk', query_head, key_blocks[distance], preferred_ele...  82.9 us
    psum x1, waiting for transfers between devices, shards(): lax.psum(jnp.dot(attention, w_out, preferred_element_type=jnp.float32), '...  73.3 us
    ppermute x8, waiting for transfers between devices, shifted(): lax.ppermute(value, axis, [(source, source + steps) for source in range(l...  53.6 us
    ppermute x8, starting transfers between devices, shifted(): lax.ppermute(value, axis, [(source, source + steps) for source in range(l...  37.8 us
    all_gather x1, waiting for transfers between devices, shards(): piece = lax.all_gather(normed, 'kv', axis=0, tiled=True)  20.5 us
    reduce_sum x4, other arithmetic, head_attention(): row_total = jnp.sum(weights, axis=2, dtype=jnp.float32)  20.3 us
    dot_general x1, matrix products, shards(): jnp.dot(attention, w_out, preferred_element_type=jnp.float32)  12.7 us
    dot_general x1, matrix products, shards(): jnp.dot(piece, w_query, preferred_element_type=jnp.float32)  10.9 us
  transfers between devices with their start and end apart: 10, of which 9 were waited for; matrix products, arithmetic and copies ran while one was open for 5% of the time, Pallas kernels for 0%

commit v1 on v0

--- a/solution.py
+++ b/solution.py
@@ -54,7 +54,10 @@
         * lax.rsqrt(jnp.mean(wide_rows * wide_rows, axis=1, keepdims=True) + norm_eps)
         * gain
     ).astype(jnp.bfloat16)
-    piece = lax.all_gather(normed, "kv", axis=0, tiled=True)
+    size = lax.axis_size("kv")
+    blocks = jnp.stack([normed for _ in range(size)])
+    blocks = lax.all_to_all(blocks, "kv", split_axis=0, concat_axis=0)
+    piece = jnp.concatenate(blocks, axis=0)
     projected = jnp.concatenate(
         [
             jnp.dot(piece, w_query, preferred_element_type=jnp.float32),

time: 375 us -> 358 us (0.955)
  waiting for transfers between devices: 148 us -> 128 us
  blocking collectives: 0 us -> 8.25 us
  matrix products: 124 us -> 119 us
    all_gather x1 -> x0, waiting for transfers between devices: 20.5 us -> none  [shards(): piece = lax.all_gather(normed, 'kv', axis=0, tiled=True)]
    all_to_all x0 -> x1, blocking collectives: none -> 8.25 us  [shards(): blocks = lax.all_to_all(blocks, 'kv', split_axis=0, concat_axis=0)]
    psum x1, waiting for transfers between devices: 73.3 us -> 79.6 us  [shards(): lax.psum(jnp.dot(attention, w_out, preferred_element_type=jnp.float32), '...]
    ppermute x8, waiting for transfers between devices: 53.6 us -> 48.8 us  [shifted(): lax.ppermute(value, axis, [(source, source + steps) for source in range(l...]
  transfers between devices with their start and end apart: 10 -> 9, of which waited for: 9 -> 8; matrix products, arithmetic and copies ran while one was open for 5% -> 5% of each run, Pallas kernels for 0% -> 0%
where the time goes in v1:
time: 358 us; the launch traced here: 357 us
  waiting for transfers between devices  128 us (36%)
  matrix products  119 us (33%)
  starting transfers between devices  37.5 us (10%)
  other arithmetic  28.9 us (8%)
  local copies, waits for them, and re-layouts  19.8 us (6%)
  between operations  14.4 us (4%)
  blocking collectives  8.25 us (2%)
    dot_general x36, matrix products, block_scores(): jnp.einsum('qgd,kd->gqk', query_head, key_blocks[distance], preferred_ele...  82.9 us
    psum x1, waiting for transfers between devices, shards(): lax.psum(jnp.dot(attention, w_out, preferred_element_type=jnp.float32), '...  79.6 us
    ppermute x8, waiting for transfers between devices, shifted(): lax.ppermute(value, axis, [(source, source + steps) for source in range(l...  48.8 us
    ppermute x8, starting transfers between devices, shifted(): lax.ppermute(value, axis, [(source, source + steps) for source in range(l...  37.5 us
    reduce_sum x4, other arithmetic, head_attention(): row_total = jnp.sum(weights, axis=2, dtype=jnp.float32)  20.3 us
    dot_general x1, matrix products, shards(): jnp.dot(attention, w_out, preferred_element_type=jnp.float32)  12.7 us
    dot_general x4, matrix products, head_attention(): jnp.einsum('gqk,kd->qgd', weights, all_values, preferred_element_type=jnp...  9.76 us
    dot_general x1, matrix products, shards(): jnp.dot(piece, w_query, preferred_element_type=jnp.float32)  9.21 us
  transfers between devices with their start and end apart: 9, of which 8 were waited for; matrix products, arithmetic and copies ran while one was open for 5% of the time, Pallas kernels for 0%

profile of v1, /device:TPU:1, one launch (start us, length us, event | category | flops | bytes accessed | tf_op | source)
XLA Modules:
  0.0 356.6 jit_solution(2982015184780136370)
XLA Ops:
  10.6 8.2 %all_to_all.5 = bf16[2,128,4096]{2,1,0:T(8,128)(2,1)S(1)} all-to-all(bf16[2,128,4096]{2,1,0:T(8,128)(2,1)S(1)} %pad_maximum_fusion), channel_id=1, replica_groups=mesh['kv'=2,'seq'=128] {'kv'}, dimensions={0} | all-to-all | bytes 4194304 | tf_op jit(solution)/shard_map/all_to_all | solution.py:59
  20.3 3.4 convolution_convert_fusion.1
  25.3 10.9 %collective-permute-done = bf16[2,256,4,128]{3,1,2,0:T(8,128)(2,1)S(1)} collective-permute-done((bf16[2,256,4,128]{3,1,2,0:T(8,128)(2,1)S(1)}, bf16[2,256,4,128]{3,1,2,0:T(8,128)(2,1)S(1)}, u32[]{:S(2)}, u32[]{:S(2)}) %collective-permute-start) | collective-permute-done | bytes 524320 | tf_op jit(solution)/shard_map/ppermute | solution.py:14
  36.1 4.1 %collective-permute-start.1 = (bf16[2,256,4,128]{3,1,2,0:T(8,128)(2,1)S(1)}, bf16[2,256,4,128]{3,1,2,0:T(8,128)(2,1)S(1)}, u32[]{:S(2)}, u32[]{:S(2)}) collective-permute-start(bf16[2,256,4,128]{3,1,2,0:T(8,128)(2,1)S(1)} %collective-permute-done), channel_id=1, source_target_pairs={{0,1},{1,2},{2,3},{3,4},{4,5},{5,6},{6,7},{7,8},{8,9},{9,10},{10,1... | collective-permute-start | bytes 1572872 | tf_op jit(solution)/shard_map/ppermute | solution.py:14
  40.3 10.0 %collective-permute-done.1 = bf16[2,256,4,128]{3,1,2,0:T(8,128)(2,1)S(1)} collective-permute-done((bf16[2,256,4,128]{3,1,2,0:T(8,128)(2,1)S(1)}, bf16[2,256,4,128]{3,1,2,0:T(8,128)(2,1)S(1)}, u32[]{:S(2)}, u32[]{:S(2)}) %collective-permute-start.1) | collective-permute-done | bytes 524320 | tf_op jit(solution)/shard_map/ppermute | solution.py:14
  51.1 4.1 %collective-permute-start.2 = (bf16[2,256,4,128]{3,1,2,0:T(8,128)(2,1)S(1)}, bf16[2,256,4,128]{3,1,2,0:T(8,128)(2,1)S(1)}, u32[]{:S(2)}, u32[]{:S(2)}) collective-permute-start(bf16[2,256,4,128]{3,1,2,0:T(8,128)(2,1)S(1)} %collective-permute-done.1), channel_id=1, source_target_pairs={{0,1},{1,2},{2,3},{3,4},{4,5},{5,6},{6,7},{7,8},{8,9},{9,10},{10,1... | collective-permute-start | bytes 1572872 | tf_op jit(solution)/shard_map/ppermute | solution.py:14
  55.2 9.1 %collective-permute-done.2 = bf16[2,256,4,128]{3,1,2,0:T(8,128)(2,1)S(1)} collective-permute-done((bf16[2,256,4,128]{3,1,2,0:T(8,128)(2,1)S(1)}, bf16[2,256,4,128]{3,1,2,0:T(8,128)(2,1)S(1)}, u32[]{:S(2)}, u32[]{:S(2)}) %collective-permute-start.2) | collective-permute-done | bytes 524320 | tf_op jit(solution)/shard_map/ppermute | solution.py:14
  64.4 4.9 %collective-permute-start.3 = (bf16[2,256,4,128]{3,1,2,0:T(8,128)(2,1)S(1)}, bf16[2,256,4,128]{3,1,2,0:T(8,128)(2,1)}, u32[]{:S(2)}, u32[]{:S(2)}) collective-permute-start(bf16[2,256,4,128]{3,1,2,0:T(8,128)(2,1)S(1)} %collective-permute-done.2), channel_id=1, source_target_pairs={{0,1},{1,2},{2,3},{3,4},{4,5},{5,6},{6,7},{7,8},{8,9},{9,10},{10,1... | collective-permute-start | bytes 1572872 | tf_op jit(solution)/shard_map/ppermute | solution.py:14
  69.3 7.5 %collective-permute-done.3 = bf16[2,256,4,128]{3,1,2,0:T(8,128)(2,1)} collective-permute-done((bf16[2,256,4,128]{3,1,2,0:T(8,128)(2,1)S(1)}, bf16[2,256,4,128]{3,1,2,0:T(8,128)(2,1)}, u32[]{:S(2)}, u32[]{:S(2)}) %collective-permute-start.3) | collective-permute-done | bytes 524320 | tf_op jit(solution)/shard_map/ppermute | solution.py:14
  76.8 5.0 %collective-permute-start.4 = (bf16[2,256,4,128]{3,1,2,0:T(8,128)(2,1)}, bf16[2,256,4,128]{3,1,2,0:T(8,128)(2,1)}, u32[]{:S(2)}, u32[]{:S(2)}) collective-permute-start(bf16[2,256,4,128]{3,1,2,0:T(8,128)(2,1)} %collective-permute-done.3), channel_id=1, source_target_pairs={{0,1},{1,2},{2,3},{3,4},{4,5},{5,6},{6,7},{7,8},{8,9},{9,10},{10,1... | collective-permute-start | bytes 1572872 | tf_op jit(solution)/shard_map/ppermute | solution.py:14
  81.8 9.2 %convolution_convert_fusion = bf16[256,2048]{1,0:T(8,128)(2,1)} fusion(bf16[256,4096]{1,0:T(8,128)(2,1)S(1)} %bitcast.285, bf16[4096,2048]{1,0:T(8,128)(2,1)} %param.12), kind=kOutput, calls=%fused_computation.106 | convolution fusion | flops 4295491584 | bytes 19922944 | tf_op jit(solution)/shard_map/dot_general | solution.py:63
  91.0 5.1 %collective-permute-start.5 = (bf16[2,256,4,128]{3,1,2,0:T(8,128)(2,1)}, bf16[2,256,4,128]{3,1,2,0:T(8,128)(2,1)}, u32[]{:S(2)}, u32[]{:S(2)}) collective-permute-start(bf16[2,256,4,128]{3,1,2,0:T(8,128)(2,1)} %collective-permute-done.4), channel_id=1, source_target_pairs={{0,1},{1,2},{2,3},{3,4},{4,5},{5,6},{6,7},{7,8},{8,9},{9,10},{10,1... | collective-permute-start | bytes 1572872 | tf_op jit(solution)/shard_map/ppermute | solution.py:14
  102.8 6.2 %collective-permute-start.6 = (bf16[2,256,4,128]{3,1,2,0:T(8,128)(2,1)}, bf16[2,256,4,128]{3,1,2,0:T(8,128)(2,1)S(1)}, u32[]{:S(2)}, u32[]{:S(2)}) collective-permute-start(bf16[2,256,4,128]{3,1,2,0:T(8,128)(2,1)} %collective-permute-done.5), channel_id=1, source_target_pairs={{0,1},{1,2},{2,3},{3,4},{4,5},{5,6},{6,7},{7,8},{8,9},{9,10},{10,1... | collective-permute-start | bytes 1572872 | tf_op jit(solution)/shard_map/ppermute | solution.py:14
  110.3 5.3 %collective-permute-done.6 = bf16[2,256,4,128]{3,1,2,0:T(8,128)(2,1)S(1)} collective-permute-done((bf16[2,256,4,128]{3,1,2,0:T(8,128)(2,1)}, bf16[2,256,4,128]{3,1,2,0:T(8,128)(2,1)S(1)}, u32[]{:S(2)}, u32[]{:S(2)}) %collective-permute-start.6) | collective-permute-done | bytes 524320 | tf_op jit(solution)/shard_map/ppermute | solution.py:14
  115.6 6.5 %collective-permute-start.7 = (bf16[2,256,4,128]{3,1,2,0:T(8,128)(2,1)S(1)}, bf16[2,256,4,128]{3,1,2,0:T(8,128)(2,1)S(1)}, u32[]{:S(2)}, u32[]{:S(2)}) collective-permute-start(bf16[2,256,4,128]{3,1,2,0:T(8,128)(2,1)S(1)} %collective-permute-done.6), channel_id=1, source_target_pairs={{0,1},{1,2},{2,3},{3,4},{4,5},{5,6},{6,7},{7,8},{8,9},{9,10},{10,1... | collective-permute-start | bytes 1572872 | tf_op jit(solution)/shard_map/ppermute | solution.py:14
  124.5 3.6 %collective-permute-done.7 = bf16[2,256,4,128]{3,1,2,0:T(8,128)(2,1)S(1)} collective-permute-done((bf16[2,256,4,128]{3,1,2,0:T(8,128)(2,1)S(1)}, bf16[2,256,4,128]{3,1,2,0:T(8,128)(2,1)S(1)}, u32[]{:S(2)}, u32[]{:S(2)}) %collective-permute-start.7) | collective-permute-done | bytes 524320 | tf_op jit(solution)/shard_map/ppermute | solution.py:14
  129.9 120.6 %while.12 = (s32[]{:T(128)}, bf16[4,256,4,128]{1,3,2,0:T(8,128)(2,1)}, bf16[4,9,256,128]{3,2,1,0:T(8,128)(2,1)S(1)}, bf16[4,9,256,128]{3,2,1,0:T(8,128)(2,1)}, b...) while((s32[]{:T(128)}, ...), condition=%wide.region_12.13_spmd.clone.clone, body=%wide.region_1.12_spmd.clone.clone.sunk | while | flops 1230764032 | bytes 72335304 | solution.py:103
  151.2 5.1 %convert_reduce_fusion.2 = f32[4,256]{1,0:T(4,128)S(1)} fusion(f32[4,256,2304]{1,2,0:T(8,128)} %get-tuple-element.530, f32[4,256]{1,0:T(4,128)S(1)} %maximum_maximum_fusion.2), kind=kLoop, calls=%fused_computation.10.clone.1 | loop fusion | flops 9436160 | bytes 9445376 | tf_op jit(solution)/shard_map/while/body/eval_jaxpr/reduce_sum | solution.py:38
  181.4 5.1 %convert_reduce_fusion.2 = f32[4,256]{1,0:T(4,128)S(1)} fusion(f32[4,256,2304]{1,2,0:T(8,128)} %get-tuple-element.530, f32[4,256]{1,0:T(4,128)S(1)} %maximum_maximum_fusion.2), kind=kLoop, calls=%fused_computation.10.clone.1 | loop fusion | flops 9436160 | bytes 9445376 | tf_op jit(solution)/shard_map/while/body/eval_jaxpr/reduce_sum | solution.py:38
  211.5 5.1 %convert_reduce_fusion.2 = f32[4,256]{1,0:T(4,128)S(1)} fusion(f32[4,256,2304]{1,2,0:T(8,128)} %get-tuple-element.530, f32[4,256]{1,0:T(4,128)S(1)} %maximum_maximum_fusion.2), kind=kLoop, calls=%fused_computation.10.clone.1 | loop fusion | flops 9436160 | bytes 9445376 | tf_op jit(solution)/shard_map/while/body/eval_jaxpr/reduce_sum | solution.py:38
  241.7 5.1 %convert_reduce_fusion.2 = f32[4,256]{1,0:T(4,128)S(1)} fusion(f32[4,256,2304]{1,2,0:T(8,128)} %get-tuple-element.530, f32[4,256]{1,0:T(4,128)S(1)} %maximum_maximum_fusion.2), kind=kLoop, calls=%fused_computation.10.clone.1 | loop fusion | flops 9436160 | bytes 9445376 | tf_op jit(solution)/shard_map/while/body/eval_jaxpr/reduce_sum | solution.py:38
  250.5 12.7 %fusion.86 = f32[256,4096]{1,0:T(8,128)} fusion(bf16[256,2048]{0,1:T(8,128)(2,1)} %bitcast.286, bf16[2048,4096]{1,0:T(8,128)(2,1)} %param.15), kind=kOutput, calls=%fused_computation.143 | convolution fusion | flops 4294967296 | bytes 22020096 | tf_op jit(solution)/shard_map/dot_general | solution.py:112
  264.7 79.6 %all-reduce.2.cloned.1.call-done = f32[256,4096]{1,0:T(8,128)} async-done(((f32[256,4096]{1,0:T(8,128)}), f32[256,4096]{1,0:T(8,128)}) %all-reduce.2.cloned.1.call-update) | async-done | bytes 4194320 | tf_op jit(solution)/shard_map/psum | solution.py:112
  347.0 2.8 fusion.74
  (117 shorter events, 123.5 us)
Async XLA Ops:
  7.2 337.1 %all-reduce.2.cloned.1.call-start = ((), (), s32[]{:S(2)}) async-start(), calls=%async_computation.1 | async-start | bytes 8388608 | tf_op jit(solution)/shard_map/psum | solution.py:112
  8.7 10.2 %copy-start.9 = (bf16[4096,512]{1,0:T(8,128)(2,1)S(1)}, bf16[4096,512]{1,0:T(8,128)(2,1)}, u32[]{:S(2)}) copy-start(bf16[4096,512]{1,0:T(8,128)(2,1)} %param.13) | copy-start | bytes 12582916
  23.8 12.3 %collective-permute-start = (bf16[2,256,4,128]{3,1,2,0:T(8,128)(2,1)S(1)}, bf16[2,256,4,128]{3,1,2,0:T(8,128)(2,1)S(1)}, u32[]{:S(2)}, u32[]{:S(2)}) collective-permute-start(bf16[2,256,4,128]{3,1,2,0:T(8,128)(2,1)S(1)} %copy_dynamic-update-slice_fusion), channel_id=1, source_target_pairs={{0,1},{1,2},{2,3},{3,4},{4,5},{5,6},{6,7},{7,8},{8,9},{9,10},{10,1... | collective-permute-start | bytes 1572872 | tf_op jit(solution)/shard_map/ppermute | solution.py:14
  36.1 28.2 %copy-start.5 = (bf16[2,256,4,128]{3,1,2,0:T(8,128)(2,1)}, bf16[2,256,4,128]{3,1,2,0:T(8,128)(2,1)S(1)}, u32[]{:S(2)}) copy-start(bf16[2,256,4,128]{3,1,2,0:T(8,128)(2,1)S(1)} %collective-permute-done) | copy-start | bytes 1572868
  36.1 14.1 %collective-permute-start.1 = (bf16[2,256,4,128]{3,1,2,0:T(8,128)(2,1)S(1)}, bf16[2,256,4,128]{3,1,2,0:T(8,128)(2,1)S(1)}, u32[]{:S(2)}, u32[]{:S(2)}) collective-permute-start(bf16[2,256,4,128]{3,1,2,0:T(8,128)(2,1)S(1)} %collective-permute-done), channel_id=1, source_target_pairs={{0,1},{1,2},{2,3},{3,4},{4,5},{5,6},{6,7},{7,8},{8,9},{9,10},{10,1... | collective-permute-start | bytes 1572872 | tf_op jit(solution)/shard_map/ppermute | solution.py:14
  50.3 0.8 copy-start.3
  51.1 13.3 %collective-permute-start.2 = (bf16[2,256,4,128]{3,1,2,0:T(8,128)(2,1)S(1)}, bf16[2,256,4,128]{3,1,2,0:T(8,128)(2,1)S(1)}, u32[]{:S(2)}, u32[]{:S(2)}) collective-permute-start(bf16[2,256,4,128]{3,1,2,0:T(8,128)(2,1)S(1)} %collective-permute-done.1), channel_id=1, source_target_pairs={{0,1},{1,2},{2,3},{3,4},{4,5},{5,6},{6,7},{7,8},{8,9},{9,10},{10,1... | collective-permute-start | bytes 1572872 | tf_op jit(solution)/shard_map/ppermute | solution.py:14
  64.4 4.9 %copy-start.7 = (bf16[2,256,4,128]{3,1,2,0:T(8,128)(2,1)}, bf16[2,256,4,128]{3,1,2,0:T(8,128)(2,1)S(1)}, u32[]{:S(2)}) copy-start(bf16[2,256,4,128]{3,1,2,0:T(8,128)(2,1)S(1)} %collective-permute-done.2) | copy-start | bytes 1572868
  64.4 12.4 %collective-permute-start.3 = (bf16[2,256,4,128]{3,1,2,0:T(8,128)(2,1)S(1)}, bf16[2,256,4,128]{3,1,2,0:T(8,128)(2,1)}, u32[]{:S(2)}, u32[]{:S(2)}) collective-permute-start(bf16[2,256,4,128]{3,1,2,0:T(8,128)(2,1)S(1)} %collective-permute-done.2), channel_id=1, source_target_pairs={{0,1},{1,2},{2,3},{3,4},{4,5},{5,6},{6,7},{7,8},{8,9},{9,10},{10,1... | collective-permute-start | bytes 1572872 | tf_op jit(solution)/shard_map/ppermute | solution.py:14
  76.8 14.2 %collective-permute-start.4 = (bf16[2,256,4,128]{3,1,2,0:T(8,128)(2,1)}, bf16[2,256,4,128]{3,1,2,0:T(8,128)(2,1)}, u32[]{:S(2)}, u32[]{:S(2)}) collective-permute-start(bf16[2,256,4,128]{3,1,2,0:T(8,128)(2,1)} %collective-permute-done.3), channel_id=1, source_target_pairs={{0,1},{1,2},{2,3},{3,4},{4,5},{5,6},{6,7},{7,8},{8,9},{9,10},{10,1... | collective-permute-start | bytes 1572872 | tf_op jit(solution)/shard_map/ppermute | solution.py:14
  91.0 9.4 %copy-start.6 = (bf16[2,256,4,128]{3,1,2,0:T(8,128)(2,1)S(1)}, bf16[2,256,4,128]{3,1,2,0:T(8,128)(2,1)}, u32[]{:S(2)}) copy-start(bf16[2,256,4,128]{3,1,2,0:T(8,128)(2,1)} %copy-done.5) | copy-start | bytes 1572868
  91.0 18.0 %copy-start.4 = (bf16[2,256,4,128]{3,1,2,0:T(8,128)(2,1)S(1)}, bf16[2,256,4,128]{3,1,2,0:T(8,128)(2,1)}, u32[]{:S(2)}) copy-start(bf16[2,256,4,128]{3,1,2,0:T(8,128)(2,1)} %copy-done.3) | copy-start | bytes 1572868
  91.0 11.8 %collective-permute-start.5 = (bf16[2,256,4,128]{3,1,2,0:T(8,128)(2,1)}, bf16[2,256,4,128]{3,1,2,0:T(8,128)(2,1)}, u32[]{:S(2)}, u32[]{:S(2)}) collective-permute-start(bf16[2,256,4,128]{3,1,2,0:T(8,128)(2,1)} %collective-permute-done.4), channel_id=1, source_target_pairs={{0,1},{1,2},{2,3},{3,4},{4,5},{5,6},{6,7},{7,8},{8,9},{9,10},{10,1... | collective-permute-start | bytes 1572872 | tf_op jit(solution)/shard_map/ppermute | solution.py:14
  99.1 10.1 %copy-start.8 = (bf16[2,256,4,128]{3,1,2,0:T(8,128)(2,1)S(1)}, bf16[2,256,4,128]{3,1,2,0:T(8,128)(2,1)}, u32[]{:S(2)}) copy-start(bf16[2,256,4,128]{3,1,2,0:T(8,128)(2,1)} %copy-done.7) | copy-start | bytes 1572868
  102.8 12.9 %collective-permute-start.6 = (bf16[2,256,4,128]{3,1,2,0:T(8,128)(2,1)}, bf16[2,256,4,128]{3,1,2,0:T(8,128)(2,1)S(1)}, u32[]{:S(2)}, u32[]{:S(2)}) collective-permute-start(bf16[2,256,4,128]{3,1,2,0:T(8,128)(2,1)} %collective-permute-done.5), channel_id=1, source_target_pairs={{0,1},{1,2},{2,3},{3,4},{4,5},{5,6},{6,7},{7,8},{8,9},{9,10},{10,1... | collective-permute-start | bytes 1572872 | tf_op jit(solution)/shard_map/ppermute | solution.py:14
  115.6 12.4 %collective-permute-start.7 = (bf16[2,256,4,128]{3,1,2,0:T(8,128)(2,1)S(1)}, bf16[2,256,4,128]{3,1,2,0:T(8,128)(2,1)S(1)}, u32[]{:S(2)}, u32[]{:S(2)}) collective-permute-start(bf16[2,256,4,128]{3,1,2,0:T(8,128)(2,1)S(1)} %collective-permute-done.6), channel_id=1, source_target_pairs={{0,1},{1,2},{2,3},{3,4},{4,5},{5,6},{6,7},{7,8},{8,9},{9,10},{10,1... | collective-permute-start | bytes 1572872 | tf_op jit(solution)/shard_map/ppermute | solution.py:14
  151.2 6.4 %copy-start = (f32[4,256,2304]{1,2,0:T(8,128)S(1)}, f32[4,256,2304]{1,2,0:T(8,128)}, u32[]{:S(2)}) copy-start(f32[4,256,2304]{1,2,0:T(8,128)} %get-tuple-element.530) | copy-start | bytes 28311556 | tf_op jit(solution)/shard_map/while
  181.3 6.4 %copy-start = (f32[4,256,2304]{1,2,0:T(8,128)S(1)}, f32[4,256,2304]{1,2,0:T(8,128)}, u32[]{:S(2)}) copy-start(f32[4,256,2304]{1,2,0:T(8,128)} %get-tuple-element.530) | copy-start | bytes 28311556 | tf_op jit(solution)/shard_map/while
  211.5 6.4 %copy-start = (f32[4,256,2304]{1,2,0:T(8,128)S(1)}, f32[4,256,2304]{1,2,0:T(8,128)}, u32[]{:S(2)}) copy-start(f32[4,256,2304]{1,2,0:T(8,128)} %get-tuple-element.530) | copy-start | bytes 28311556 | tf_op jit(solution)/shard_map/while
  241.7 6.4 %copy-start = (f32[4,256,2304]{1,2,0:T(8,128)S(1)}, f32[4,256,2304]{1,2,0:T(8,128)}, u32[]{:S(2)}) copy-start(f32[4,256,2304]{1,2,0:T(8,128)} %get-tuple-element.530) | copy-start | bytes 28311556 | tf_op jit(solution)/shard_map/while
  263.1 0.7 copy-start.10
  263.2 83.8 %copy-start.1 = (bf16[128,4096]{1,0:T(8,128)(2,1)S(1)}, bf16[128,4096]{1,0:T(8,128)(2,1)}, u32[]{:S(2)}) copy-start(bf16[128,4096]{1,0:T(8,128)(2,1)} %param.10) | copy-start | bytes 3145732
  264.6 85.1 %copy-start.2 = (bf16[2,2,4,128,128]{4,3,2,1,0:T(8,128)(2,1)}, bf16[2,2,4,128,128]{4,3,2,1,0:T(8,128)(2,1)S(1)}, u32[]{:S(2)}) copy-start(bf16[2,2,4,128,128]{4,3,2,1,0:T(8,128)(2,1)S(1)} %scatter_fusion) | copy-start | bytes 1572868
Sparse Core Ops, SparseCore 0:
  263.3 80.9 all-reduce.1
